TPU v7x, 256 devices: a whole 4x4x8 slice. The times are simulated.
256 devices in a mesh: blk: 64 (over y_lo, x, z), states: 4 (over y_hi, core).
Axes of the slice: x: 4, y: 4 (y_hi: 2, y_lo: 2; y = y_hi * 2 + y_lo), z: 8, core: 2. Of those that a mesh axis runs over, the one named last changes fastest.
Arguments:
- start_states: float32 [128, 16, 128, 512], P('blk', None, None, 'states'), may hold values from -6 to 6
- couplings: float32 [16, 128, 128], replicated, may hold values from -0.1875 to 0.1875
- potential: float32 [128, 16, 128], P('blk'), may hold values from -18 to 18
- site_offsets: int32 [128, 6, 16], P('blk'), may hold values from 0 to 15
- coupling_index: int32 [128, 7, 16], P('blk'), may hold values from 0 to 15
- degrees: int32 [512], P('states'), may hold values from 1 to 3, as said below
Outputs:
- orthonormal: float32 [128, 16, 128, 512], P('blk', 'states')
Inputs may be any that keep to these rules, and one draw needn't show every extreme that they name: `degrees`: every degree from 1 to 3 belongs to some state.
All inputs are finite; a program needn't handle non-finite values.
Results may differ from a plain program's by a relative error of at most 0.0003.
Values sent between devices are 32-bit elements; how exact they have to be, the bound alone decides.
A program may use at most 128 MiB of HBM per device.

v0:
```python
import jax
import jax.numpy as jnp
from jax import lax
from jax.sharding import PartitionSpec as P

cut_share = 0.3
exact = lax.Precision.HIGHEST


def padded_2(shard, sides, width):
    for axis, dim in sides:
        devices, length = (lax.axis_size(axis), shard.shape[dim])
        up = [(i, (i + 1) % devices) for i in range(devices)]
        down = [(j, i) for i, j in up]
        last = lax.slice_in_dim(shard, length - width, length, axis=dim)
        first = lax.slice_in_dim(shard, 0, width, axis=dim)
        before = lax.ppermute(last, axis, up)
        after = lax.ppermute(first, axis, down)
        shard = jnp.concatenate([before, shard, after], axis=dim)
    return shard


def copy_for_each(shard, axis):
    copies = jnp.broadcast_to(shard, (lax.axis_size(axis), *shard.shape))
    return lax.all_to_all(copies, axis, split_axis=0, concat_axis=0, tiled=True)


def folded_in_pairs(pieces, combine):
    while len(jax.tree.leaves(pieces)[0]) > 1:
        pieces = jax.vmap(combine)(
            *(jax.tree.map(lambda part: part[side::2], pieces) for side in (0, 1))
        )
    return jax.tree.map(lambda part: part[0], pieces)


def joined_all(shard, axis, combine):
    pieces = jax.tree.map(lambda part: copy_for_each(part, axis), shard)
    return folded_in_pairs(pieces, combine)


def coupling_blocks(couplings, index_rows):
    return jnp.take(couplings, index_rows, axis=0)


def apply_inner(padded, blocks_used, onsite, offset_rows):
    middle = padded[1:-1]
    lower_layers = padded[:-2]
    upper_layers = padded[2:]
    count = onsite.shape[1]
    site_ids = jnp.arange(count, dtype=jnp.int32)
    layer_ids = jnp.arange(middle.shape[0], dtype=jnp.int32)
    pieces = [middle]
    for slot in range(1, 7):
        if slot == 5:
            source = lower_layers
        elif slot == 6:
            source = upper_layers
        else:
            source = middle
        neighbour = (site_ids[None, :] + offset_rows[:, slot - 1, :]) % count
        pieces.append(source[layer_ids[:, None], neighbour])
    stacked = jnp.stack(pieces, axis=1)
    summed = jnp.einsum("lksij,lksjn->lsin", blocks_used, stacked, precision=exact)
    return summed + onsite[..., None] * middle


def extrema_of(couplings, onsite, index_rows):
    row_abs = jnp.sum(jnp.abs(couplings), axis=2)
    diag_all = jnp.diagonal(couplings, axis1=1, axis2=2)
    table_ids = jnp.arange(couplings.shape[0], dtype=jnp.int32)
    onehot = (index_rows[..., None] == table_ids).astype(jnp.float32)
    picked_abs = jnp.einsum("lksc,ci->lksi", onehot, row_abs, precision=exact)
    picked_diag = jnp.einsum("lsc,ci->lsi", onehot[:, 0], diag_all, precision=exact)
    centers = picked_diag + onsite
    radii = picked_abs[:, 0] - jnp.abs(picked_diag) + jnp.sum(picked_abs[:, 1:], axis=1)
    return (jnp.max(centers + radii), jnp.min(centers - radii))


def combine(first, second):
    return (jnp.maximum(first[0], second[0]), jnp.minimum(first[1], second[1]))


def faces(field):
    return padded_2(field, (("blk", 0),), 1)


def per_device(start_states, couplings, potential, site_offsets, coupling_index, degrees):
    upper, lower = joined_all(extrema_of(couplings, potential, coupling_index), "blk", combine)
    cut_edge = lower + cut_share * (upper - lower)
    middle_value = (upper + cut_edge) / 2.0
    half_width = (upper - cut_edge) / 2.0

    def scaled(applied, field):
        return (applied - middle_value * field) / half_width

    local_blocks = coupling_blocks(couplings, coupling_index)
    first_step = scaled(
        apply_inner(faces(start_states), local_blocks, potential, site_offsets), start_states
    )
    second = (
        2.0
        * scaled(apply_inner(faces(first_step), local_blocks, potential, site_offsets), first_step)
        - start_states
    )
    third = (
        2.0 * scaled(apply_inner(faces(second), local_blocks, potential, site_offsets), second)
        - first_step
    )
    chosen = jnp.where(degrees == 1, first_step, jnp.where(degrees == 2, second, third))
    regrouped = lax.all_to_all(chosen, "states", split_axis=1, concat_axis=3, tiled=True)
    rows = regrouped.reshape(-1, regrouped.shape[-1])
    partial_gram = lax.dot_general(
        rows, rows, (((0,), (0,)), ((), ())), precision=exact, preferred_element_type=jnp.float32
    )
    gram = lax.psum(partial_gram, ("blk", "states"))
    factor = jnp.linalg.cholesky(gram)
    identity = jnp.eye(gram.shape[0], dtype=jnp.float32)
    inverse_factor = jax.scipy.linalg.solve_triangular(factor, identity, lower=True)
    orthonormal = jnp.dot(
        rows, inverse_factor.T, precision=exact, preferred_element_type=jnp.float32
    )
    return orthonormal.reshape(regrouped.shape)


def solution(mesh):
    in_specs = (
        P("blk", None, None, "states"),
        P(),
        P("blk", None, None),
        P("blk", None, None),
        P("blk", None, None),
        P("states"),
    )
    out_specs = P("blk", "states", None, None)
    return jax.shard_map(
        per_device, mesh=mesh, in_specs=in_specs, out_specs=out_specs, check_vma=False
    )
```

profile of v0, /device:TPU:2, one launch (start us, length us, event | category | flops | bytes accessed | tf_op | source)
XLA Modules:
  0.0 722.4 jit_solution(9385407167922655574)
XLA Ops:
  8.1 6.1 copy.46
  14.7 1.8 gather_fusion.7
  18.6 13.0 %all-to-all-start = ((f32[64,1,1]{2,1,0:T(1,128)}), f32[64,1,1]{2,1,0:T(1,128)S(1)}, u32[]{:S(2)}, u32[]{:S(2)}) async-start(f32[64,1,1]{2,1,0:T(1,128)} %broadcast_in_dim.49), calls=%async_computation | async-start | bytes 65536 | tf_op jit(solution)/shard_map/all_to_all | solution.py:25
  33.2 2.7 collective-permute-start.1
  37.5 2.0 gather_fusion.1
  39.6 2.0 gather_fusion.2
  41.7 2.0 gather_fusion.3
  43.8 2.0 gather_fusion.4
  45.9 3.4 constant_dynamic-update-slice_fusion.5
  55.6 6.7 gather_fusion
  63.7 12.0 %all-to-all-start.1 = ((f32[64,1,1]{2,1,0:T(1,128)}), f32[64,1,1]{2,1,0:T(1,128)S(1)}, u32[]{:S(2)}, u32[]{:S(2)}) async-start(f32[64,1,1]{2,1,0:T(1,128)} %broadcast_in_dim.50), calls=%async_computation.1 | async-start | bytes 65536 | tf_op jit(solution)/shard_map/all_to_all | solution.py:25
  77.5 7.6 %all-to-all-done.1 = f32[64,1,1]{2,1,0:T(1,128)S(1)} async-done(((f32[64,1,1]{2,1,0:T(1,128)}), f32[64,1,1]{2,1,0:T(1,128)S(1)}, u32[]{:S(2)}, u32[]{:S(2)}) %all-to-all-start.1) | async-done | bytes 288 | tf_op jit(solution)/shard_map/all_to_all | solution.py:25
  90.6 4.1 pad_maximum_fusion.4
  94.7 3.6 gather_fusion.5
  98.3 3.1 constant_dynamic-update-slice_fusion.1
  101.4 3.6 gather_fusion.6
  105.0 3.1 constant_dynamic-update-slice_fusion
  108.1 21.0 %bitcast_dynamic-update-slice_fusion.2 = (f32[2,7,16,128,128]{4,3,2,0,1:T(8,128)}, f32[2,16,128,128]{3,2,1,0:T(8,128)S(1)}) fusion(f32[]{:T(128)S(6)} %div.29, f32[2,16,128,128]{3,2,1,0:T(8,128)S(1)} %copy-done.1, f32[]{:T(128)S(6)} %div.28, f32[2,16,128]{2,1,0:T(8,128)S(1)} %copy-done.22, f32[2,7,16,128,128]{4,3,1,2,0:T(8,128)} %constant_dynamic-update-slice_fusion, ...), kind=kOutput, calls=%fused_computation.56 | convolution fusion | flops 5643436032 | bytes 35668200 | tf_op jit(solution)/shard_map/lksij,lksjn->lsin/dot_general | solution.py:63
  129.2 1.8 fusion.106
  131.2 1.7 collective-permute-start.3
  133.6 3.6 gather_fusion.8
  137.2 3.6 gather_fusion.9
  140.8 3.6 gather_fusion.10
  144.4 3.6 gather_fusion.11
  148.0 3.3 constant_dynamic-update-slice_fusion.11
  158.3 3.6 pad_maximum_fusion.2
  161.9 3.6 gather_fusion.12
  165.5 3.6 gather_fusion.13
  169.1 3.3 constant_dynamic-update-slice_fusion.7
  173.9 21.6 %bitcast_dynamic-update-slice_fusion.1 = (f32[2,7,16,128,128]{4,3,2,0,1:T(8,128)}, f32[2,16,128,128]{3,2,1,0:T(8,128)}) fusion(f32[2,16,128,128]{3,2,1,0:T(8,128)S(1)} %copy-done.1, f32[]{:T(128)S(6)} %div.29, f32[2,16,128,128]{3,2,1,0:T(8,128)} %copy-done.2, f32[]{:T(128)S(6)} %div.28, f32[2,16,128]{2,1,0:T(8,128)S(1)} %copy-done.22, ...), kind=kOutput, calls=%fused_computation.50 | convolution fusion | flops 5644484608 | bytes 37765352 | tf_op jit(solution)/shard_map/lksij,lksjn->lsin/dot_general | solution.py:63
  195.5 2.9 fusion.105
  198.4 3.8 collective-permute-start.5
  202.4 2.0 gather_fusion.14
  204.4 2.1 gather_fusion.15
  206.4 2.0 gather_fusion.16
  208.4 2.0 gather_fusion.17
  210.5 3.3 constant_dynamic-update-slice_fusion.17
  219.9 1.8 collective-permute-done.5
  221.8 4.3 collective-permute-done.4
  226.0 4.0 pad_maximum_fusion
  230.0 2.3 gather_fusion.18
  232.3 3.6 gather_fusion.19
  235.9 1.6 constant_dynamic-update-slice_fusion.13
  241.2 21.2 %fusion.19 = f32[2,16,128,128]{3,2,1,0:T(8,128)} fusion(f32[2,16,128,128]{3,2,1,0:T(8,128)S(1)} %copy-done.4, f32[2,16,128,128]{3,2,1,0:T(8,128)S(1)} %copy-done.6, f32[2,7,16,128,128]{4,3,2,0,1:T(8,128)} %constant_dynamic-update-slice_fusion.12, f32[2,7,16,128,128]{4,3,2,1,0:T(8,128)} %bitcast.190, pred[2,7,16]{1,2,0:T(8,128)(4,1)S(1)} %copy.43, ...), kind=kOutput, calls=%fused_computation.49 | convolution fusion | flops 5645533184 | bytes 35668456 | tf_op jit(solution)/shard_map/lksij,lksjn->lsin/dot_general | solution.py:63
  262.4 1.8 copy.52
  264.2 31.1 %all_to_all.33 = f32[2,16,128,128]{3,2,0,1:T(8,128)S(1)} all-to-all(f32[2,16,128,128]{3,2,0,1:T(8,128)S(1)} %copy.52), channel_id=1, replica_groups=mesh['blk'=64,'states'=4] {'states'}, dimensions={1} | all-to-all | bytes 4194304 | tf_op jit(solution)/shard_map/all_to_all | solution.py:110
  296.7 4.5 fusion.11
  303.1 2.5 dot_general.28
  305.6 250.9 %all-reduce.3.cloned.1.call-done = f32[512,512]{0,1:T(8,128)} async-done(((f32[512,512]{0,1:T(8,128)}), f32[512,512]{0,1:T(8,128)}) %all-reduce.3.cloned.1.call-update) | async-done | bytes 1048592 | tf_op jit(solution)/shard_map/psum | solution.py:115
  556.5 2.6 copy.55
  561.6 11.7 %cholesky.104 = f32[128,128]{1,0:T(8,128)S(1)} custom-call(f32[128,128]{1,0:T(8,128)S(1)} %cholesky.266), custom_call_target="Cholesky" | custom-call | tf_op jit(solution)/shard_map/jit(cholesky)/cholesky | solution.py:116
  573.5 9.8 %custom-call.31 = f32[1,128,128]{1,2,0:T(8,128)S(1)} custom-call(f32[1,128,128]{2,1,0:T(8,128)S(1)} %get-tuple-element.48), custom_call_target="InvertDiagBlocksLowerTriangular" | custom-call | tf_op jit(solution)/shard_map/jit(cholesky)/cholesky | solution.py:116
  585.8 11.7 %cholesky.217 = f32[128,128]{1,0:T(8,128)S(1)} custom-call(f32[128,128]{1,0:T(8,128)S(1)} %cholesky.270), custom_call_target="Cholesky" | custom-call | tf_op jit(solution)/shard_map/jit(cholesky)/cholesky | solution.py:116
  597.5 10.0 %custom-call.32 = f32[1,128,128]{1,2,0:T(8,128)S(1)} custom-call(f32[1,128,128]{2,1,0:T(8,128)S(1)} %get-tuple-element.45), custom_call_target="InvertDiagBlocksLowerTriangular" | custom-call | tf_op jit(solution)/shard_map/jit(cholesky)/cholesky | solution.py:116
  609.1 11.7 %cholesky.238 = f32[128,128]{1,0:T(8,128)S(1)} custom-call(f32[128,128]{1,0:T(8,128)S(1)} %cholesky.275), custom_call_target="Cholesky" | custom-call | tf_op jit(solution)/shard_map/jit(cholesky)/cholesky | solution.py:116
  620.8 9.8 %custom-call.33 = f32[1,128,128]{1,2,0:T(8,128)S(1)} custom-call(f32[1,128,128]{2,1,0:T(8,128)S(1)} %get-tuple-element.42), custom_call_target="InvertDiagBlocksLowerTriangular" | custom-call | tf_op jit(solution)/shard_map/jit(cholesky)/cholesky | solution.py:116
  632.1 11.7 %cholesky.255 = f32[128,128]{1,0:T(8,128)S(1)} custom-call(f32[128,128]{1,0:T(8,128)S(1)} %convolution_subtract_fusion.5), custom_call_target="Cholesky" | custom-call | tf_op jit(solution)/shard_map/jit(cholesky)/cholesky | solution.py:116
  649.7 13.9 %while.1 = (s32[]{:T(128)}, f32[512,512]{1,0:T(8,128)}, s32[4,2]{0,1:T(2,128)S(1)}, f32[4,128,128]{2,1,0:T(8,128)}, s32[]{:T(128)}) while((s32[]{:T(128)}, f32[512,512]{1,0:T(8,128)}, s32[4,2]{0,1:T(2,128)S(1)}, f32[4,128,128]{2,1,0:T(8,128)}, s32[]{:T(128)}) %tuple.46), condition=%wide.while_cond, body=%wide.while_body.sunk | while | flops 2 | bytes 132205 | solution.py:118
  650.4 2.9 bitcast_dynamic-update-slice_fusion.5
  653.9 2.9 bitcast_dynamic-update-slice_fusion.5
  657.4 2.9 bitcast_dynamic-update-slice_fusion.5
  660.9 2.8 bitcast_dynamic-update-slice_fusion.5
  663.7 40.1 %custom-call.34 = f32[4,128,128]{1,2,0:T(8,128)S(1)} custom-call(f32[4,128,128]{2,1,0:T(8,128)} %get-tuple-element.12), custom_call_target="InvertDiagBlocksLowerTriangular" | custom-call | tf_op jit(solution)/shard_map/jit(_solve_triangular)/triangular_solve | solution.py:118
  710.5 4.8 fusion.30
  (171 shorter events, 63.5 us)
Async XLA Ops:
  8.1 6.2 copy-start.23
  8.1 8.3 %copy-start.22 = (f32[2,16,128]{2,1,0:T(8,128)S(1)}, f32[2,16,128]{2,1,0:T(8,128)}, u32[]{:S(2)}) copy-start(f32[2,16,128]{2,1,0:T(8,128)} %param.8) | copy-start | bytes 49156
  8.1 23.5 %copy-start.1 = (f32[2,16,128,128]{3,2,1,0:T(8,128)S(1)}, f32[2,16,128,128]{3,2,1,0:T(8,128)}, u32[]{:S(2)}) copy-start(f32[2,16,128,128]{3,2,1,0:T(8,128)} %param.6) | copy-start | bytes 6291460
  18.6 43.8 %all-to-all-start = ((f32[64,1,1]{2,1,0:T(1,128)}), f32[64,1,1]{2,1,0:T(1,128)S(1)}, u32[]{:S(2)}, u32[]{:S(2)}) async-start(f32[64,1,1]{2,1,0:T(1,128)} %broadcast_in_dim.49), calls=%async_computation | async-start | bytes 65536 | tf_op jit(solution)/shard_map/all_to_all | solution.py:25
  33.2 57.4 %collective-permute-start.1 = (f32[1,16,128,128]{3,2,1,0:T(8,128)}, f32[1,16,128,128]{3,2,1,0:T(8,128)}, u32[]{:S(2)}, u32[]{:S(2)}) collective-permute-start(f32[1,16,128,128]{3,2,1,0:T(8,128)} %get-tuple-element.37), channel_id=1, source_target_pairs={{4,0},{8,4},{12,8},{16,12},{20,16},{24,20},{28,24},{32,28},{36,32}... | collective-permute-start | bytes 3145736 | tf_op jit(solution)/shard_map/ppermute | solution.py:18
  35.9 1.5 copy-start.24
  35.9 54.7 %collective-permute-start = (f32[1,16,128,128]{3,2,1,0:T(8,128)}, f32[1,16,128,128]{3,2,1,0:T(8,128)}, u32[]{:S(2)}, u32[]{:S(2)}) collective-permute-start(f32[1,16,128,128]{3,2,1,0:T(8,128)} %get-tuple-element.38), channel_id=1, source_target_pairs={{0,4},{4,8},{8,12},{12,16},{16,20},{20,24},{24,28},{28,32},{32,36}... | collective-permute-start | bytes 3145736 | tf_op jit(solution)/shard_map/ppermute | solution.py:17
  45.9 3.4 copy-start.8
  49.3 2.3 copy-start.9
  51.6 2.3 copy-start.10
  54.0 1.6 copy-start
  63.7 21.4 %all-to-all-start.1 = ((f32[64,1,1]{2,1,0:T(1,128)}), f32[64,1,1]{2,1,0:T(1,128)S(1)}, u32[]{:S(2)}, u32[]{:S(2)}) async-start(f32[64,1,1]{2,1,0:T(1,128)} %broadcast_in_dim.50), calls=%async_computation.1 | async-start | bytes 65536 | tf_op jit(solution)/shard_map/all_to_all | solution.py:25
  75.6 480.9 %all-reduce.3.cloned.1.call-start = ((), (), s32[]{:S(2)}) async-start(), calls=%async_computation.3 | async-start | bytes 2097152 | tf_op jit(solution)/shard_map/psum | solution.py:115
  129.2 2.0 copy-start.2
  131.2 26.2 %collective-permute-start.3 = (f32[1,16,128,128]{3,2,1,0:T(8,128)}, f32[1,16,128,128]{3,2,1,0:T(8,128)S(1)}, u32[]{:S(2)}, u32[]{:S(2)}) collective-permute-start(f32[1,16,128,128]{3,2,1,0:T(8,128)} %get-tuple-element.33), channel_id=1, source_target_pairs={{4,0},{8,4},{12,8},{16,12},{20,16},{24,20},{28,24},{32,28},{36,32}... | collective-permute-start | bytes 3145736 | tf_op jit(solution)/shard_map/ppermute | solution.py:18
  132.9 24.9 %collective-permute-start.2 = (f32[1,16,128,128]{3,2,1,0:T(8,128)}, f32[1,16,128,128]{3,2,1,0:T(8,128)}, u32[]{:S(2)}, u32[]{:S(2)}) collective-permute-start(f32[1,16,128,128]{3,2,1,0:T(8,128)} %get-tuple-element.34), channel_id=1, source_target_pairs={{0,4},{4,8},{8,12},{12,16},{16,20},{20,24},{24,28},{28,32},{32,36}... | collective-permute-start | bytes 3145736 | tf_op jit(solution)/shard_map/ppermute | solution.py:17
  148.0 3.3 copy-start.16
  151.2 2.3 copy-start.15
  153.6 2.3 copy-start.12
  155.9 2.3 copy-start.3
  169.0 3.3 copy-start.18
  195.5 6.8 copy-start.25
  195.5 6.8 copy-start.5
  198.4 23.4 %collective-permute-start.5 = (f32[1,16,128,128]{3,2,1,0:T(8,128)}, f32[1,16,128,128]{3,2,1,0:T(8,128)}, u32[]{:S(2)}, u32[]{:S(2)}) collective-permute-start(f32[1,16,128,128]{3,2,1,0:T(8,128)} %get-tuple-element.29), channel_id=1, source_target_pairs={{4,0},{8,4},{12,8},{16,12},{20,16},{24,20},{28,24},{32,28},{36,32}... | collective-permute-start | bytes 3145736 | tf_op jit(solution)/shard_map/ppermute | solution.py:18
  202.2 23.9 %collective-permute-start.4 = (f32[1,16,128,128]{3,2,1,0:T(8,128)S(1)}, f32[1,16,128,128]{3,2,1,0:T(8,128)}, u32[]{:S(2)}, u32[]{:S(2)}) collective-permute-start(f32[1,16,128,128]{3,2,1,0:T(8,128)S(1)} %get-tuple-element.30), channel_id=1, source_target_pairs={{0,4},{4,8},{8,12},{12,16},{16,20},{20,24},{24,28},{28,32},{32,36}... | collective-permute-start | bytes 3145736 | tf_op jit(solution)/shard_map/ppermute | solution.py:17
  210.5 3.3 copy-start.14
  213.8 2.3 copy-start.13
  216.1 2.3 copy-start.11
  235.9 2.3 copy-start.17
  238.2 2.3 copy-start.4
  238.2 3.0 copy-start.6
  296.7 4.5 copy-start.7
  556.5 2.6 copy-start.19
  560.6 1.0 copy-start.21
  649.7 57.0 %copy-start.20 = (f32[512,512]{1,0:T(8,128)S(1)}, f32[512,512]{1,0:T(8,128)}, u32[]{:S(2)}) copy-start(f32[512,512]{1,0:T(8,128)} %fusion.46) | copy-start | bytes 3145732
Sparse Core Ops, SparseCore 0:
  301.3 255.1 all-reduce.2
where the time goes:
time: 730 us; the launch traced here: 722 us
  waiting for transfers between devices  265 us (36%)
  local copies, waits for them, and re-layouts  148 us (20%)
  other arithmetic  138 us (19%)
  matrix products  86.3 us (12%)
  starting transfers between devices  34.2 us (5%)
  blocking collectives  31.1 us (4%)
  between operations  19.3 us (3%)
    psum x1, waiting for transfers between devices, per_device(): gram = lax.psum(partial_gram, ('blk', 'states'))  251 us
    another operation x14, other arithmetic, per_device(): factor = jnp.linalg.cholesky(gram)  78.6 us
    dot_general x3, matrix products, apply_inner(): jnp.einsum('lksij,lksjn->lsin', blocks_used, stacked, precision=exact)  63.8 us
    gather x18, local copies, waits for them, and re-layouts, apply_inner(): pieces.append(source[layer_ids[:, None], neighbour])  50.7 us
    unnamed x69, local copies, waits for them, and re-layouts  48.1 us
    another operation x3, other arithmetic, per_device(): jax.scipy.linalg.solve_triangular(factor, identity, lower=True)  41.4 us
    all_to_all x1, blocking collectives, per_device(): lax.all_to_all(chosen, 'states', split_axis=1, concat_axis=3, tiled=True)  31.1 us
    all_to_all x2, starting transfers between devices, copy_for_each(): return lax.all_to_all(copies, axis, split_axis=0, concat_axis=0, tiled=True)  25 us
  transfers between devices with their start and end apart: 9, of which 5 were waited for; matrix products, arithmetic and copies ran while one was open for 10% of the time, Pallas kernels for 0%

commit v1 on v0

--- a/solution.py
+++ b/solution.py
@@ -112,7 +112,7 @@
     partial_gram = lax.dot_general(
         rows, rows, (((0,), (0,)), ((), ())), precision=exact, preferred_element_type=jnp.float32
     )
-    gram = lax.psum(partial_gram, ("blk", "states"))
+    gram = lax.psum(lax.psum(partial_gram, "blk"), "states")
     factor = jnp.linalg.cholesky(gram)
     identity = jnp.eye(gram.shape[0], dtype=jnp.float32)
     inverse_factor = jax.scipy.linalg.solve_triangular(factor, identity, lower=True)

time: 730 us -> 1140 us (1.56)
  waiting for transfers between devices: 265 us -> 667 us
    psum x1 -> x2, waiting for transfers between devices: 251 us -> 653 us  [per_device(): gram = lax.psum(lax.psum(partial_gram, 'blk'), 'states')]
    unnamed x69 -> x65, local copies, waits for them, and re-layouts: 48.1 us -> 48.4 us
  transfers between devices with their start and end apart: 9 -> 10, of which waited for: 5 -> 6; matrix products, arithmetic and copies ran while one was open for 10% -> 7% of each run, Pallas kernels for 0% -> 0%
where the time goes in v1:
time: 1140 us; the launch traced here: 1130 us
  waiting for transfers between devices  667 us (59%)
  local copies, waits for them, and re-layouts  151 us (13%)
  other arithmetic  138 us (12%)
  matrix products  86.7 us (8%)
  starting transfers between devices  34.3 us (3%)
  blocking collectives  31.1 us (3%)
  between operations  19.1 us (2%)
    psum x2, waiting for transfers between devices, per_device(): gram = lax.psum(lax.psum(partial_gram, 'blk'), 'states')  653 us
    another operation x14, other arithmetic, per_device(): factor = jnp.linalg.cholesky(gram)  78.6 us
    dot_general x3, matrix products, apply_inner(): jnp.einsum('lksij,lksjn->lsin', blocks_used, stacked, precision=exact)  64.3 us
    gather x18, local copies, waits for them, and re-layouts, apply_inner(): pieces.append(source[layer_ids[:, None], neighbour])  52 us
    unnamed x65, local copies, waits for them, and re-layouts  48.4 us
    another operation x3, other arithmetic, per_device(): jax.scipy.linalg.solve_triangular(factor, identity, lower=True)  41.4 us
    all_to_all x1, blocking collectives, per_device(): lax.all_to_all(chosen, 'states', split_axis=1, concat_axis=3, tiled=True)  31.1 us
    all_to_all x2, starting transfers between devices, copy_for_each(): return lax.all_to_all(copies, axis, split_axis=0, concat_axis=0, tiled=True)  25 us
  transfers between devices with their start and end apart: 10, of which 6 were waited for; matrix products, arithmetic and copies ran while one was open for 7% of the time, Pallas kernels for 0%

profile of v1, /device:TPU:2, one launch (start us, length us, event | category | flops | bytes accessed | tf_op | source)
XLA Modules:
  0.0 1128.2 jit_solution(15060743339823348759)
XLA Ops:
  8.1 6.1 copy.46
  14.7 1.8 gather_fusion.7
  18.6 13.0 %all-to-all-start = ((f32[64,1,1]{2,1,0:T(1,128)}), f32[64,1,1]{2,1,0:T(1,128)S(1)}, u32[]{:S(2)}, u32[]{:S(2)}) async-start(f32[64,1,1]{2,1,0:T(1,128)} %broadcast_in_dim.49), calls=%async_computation | async-start | bytes 65536 | tf_op jit(solution)/shard_map/all_to_all | solution.py:25
  33.1 2.7 collective-permute-start.1
  37.4 2.0 gather_fusion.1
  39.5 2.0 gather_fusion.2
  41.6 2.0 gather_fusion.3
  43.7 2.0 gather_fusion.4
  45.8 3.3 constant_dynamic-update-slice_fusion.5
  55.5 6.7 gather_fusion
  63.5 12.0 %all-to-all-start.1 = ((f32[64,1,1]{2,1,0:T(1,128)}), f32[64,1,1]{2,1,0:T(1,128)S(1)}, u32[]{:S(2)}, u32[]{:S(2)}) async-start(f32[64,1,1]{2,1,0:T(1,128)} %broadcast_in_dim.50), calls=%async_computation.1 | async-start | bytes 65536 | tf_op jit(solution)/shard_map/all_to_all | solution.py:25
  77.4 7.6 all-to-all-done.1
  90.3 3.9 pad_maximum_fusion.4
  94.2 3.6 gather_fusion.5
  97.8 3.1 constant_dynamic-update-slice_fusion.1
  100.9 3.6 gather_fusion.6
  104.5 3.1 constant_dynamic-update-slice_fusion
  107.7 21.4 %bitcast_dynamic-update-slice_fusion.2 = (f32[2,7,16,128,128]{4,3,2,0,1:T(8,128)}, f32[2,16,128,128]{3,2,1,0:T(8,128)}) fusion(f32[]{:T(128)S(6)} %div.29, f32[2,16,128,128]{3,2,1,0:T(8,128)S(1)} %copy-done.1, f32[]{:T(128)S(6)} %div.28, f32[2,16,128]{2,1,0:T(8,128)S(1)} %copy-done.20, f32[2,7,16,128,128]{4,3,1,2,0:T(8,128)} %constant_dynamic-update-slice_fusion, ...), kind=kOutput, calls=%fused_computation.56 | convolution fusion | flops 5643436032 | bytes 35668200 | tf_op jit(solution)/shard_map/lksij,lksjn->lsin/dot_general | solution.py:63
  129.1 2.8 fusion.106
  134.3 3.6 gather_fusion.8
  137.9 3.6 gather_fusion.9
  141.5 3.6 gather_fusion.10
  145.1 3.6 gather_fusion.11
  148.6 3.3 constant_dynamic-update-slice_fusion.11
  158.9 4.0 pad_maximum_fusion.2
  163.0 3.6 gather_fusion.12
  166.6 3.6 gather_fusion.13
  170.1 3.3 constant_dynamic-update-slice_fusion.7
  175.0 21.6 %bitcast_dynamic-update-slice_fusion.1 = (f32[2,7,16,128,128]{4,3,2,0,1:T(8,128)}, f32[2,16,128,128]{3,2,1,0:T(8,128)}) fusion(f32[2,16,128,128]{3,2,1,0:T(8,128)S(1)} %copy-done.1, f32[]{:T(128)S(6)} %div.29, f32[2,16,128,128]{3,2,1,0:T(8,128)} %get-tuple-element.62, f32[]{:T(128)S(6)} %div.28, f32[2,16,128]{2,1,0:T(8,128)S(1)} %copy-done.20, ...), kind=kOutput, calls=%fused_computation.50 | convolution fusion | flops 5644484608 | bytes 37765352 | tf_op jit(solution)/shard_map/lksij,lksjn->lsin/dot_general | solution.py:63
  196.6 3.2 fusion.105
  199.8 3.8 collective-permute-start.5
  203.8 2.0 gather_fusion.14
  205.8 2.1 gather_fusion.15
  207.9 2.0 gather_fusion.16
  209.9 2.0 gather_fusion.17
  211.9 3.3 constant_dynamic-update-slice_fusion.17
  221.4 1.9 collective-permute-done.5
  223.3 4.5 collective-permute-done.4
  227.7 4.0 pad_maximum_fusion
  231.7 3.6 gather_fusion.18
  235.3 3.6 gather_fusion.19
  238.9 3.3 constant_dynamic-update-slice_fusion.13
  244.6 21.2 %fusion.19 = f32[2,16,128,128]{3,2,1,0:T(8,128)} fusion(f32[2,16,128,128]{3,2,1,0:T(8,128)S(1)} %copy-done.3, f32[2,16,128,128]{3,2,1,0:T(8,128)S(1)} %copy-done.4, f32[2,7,16,128,128]{4,3,2,0,1:T(8,128)} %constant_dynamic-update-slice_fusion.12, f32[2,7,16,128,128]{4,3,2,1,0:T(8,128)} %bitcast.190, pred[2,7,16]{1,2,0:T(8,128)(4,1)S(1)} %copy.43, ...), kind=kOutput, calls=%fused_computation.49 | convolution fusion | flops 5645533184 | bytes 35668456 | tf_op jit(solution)/shard_map/lksij,lksjn->lsin/dot_general | solution.py:63
  265.8 1.7 copy.52
  267.5 31.1 %all_to_all.33 = f32[2,16,128,128]{3,2,0,1:T(8,128)S(1)} all-to-all(f32[2,16,128,128]{3,2,0,1:T(8,128)S(1)} %copy.52), channel_id=1, replica_groups=mesh['blk'=64,'states'=4] {'states'}, dimensions={1} | all-to-all | bytes 4194304 | tf_op jit(solution)/shard_map/all_to_all | solution.py:110
  300.0 4.5 fusion.11
  304.6 597.3 %all-reduce.4.cloned.1.call-done = f32[512,512]{0,1:T(8,128)} async-done(((f32[512,512]{0,1:T(8,128)}), f32[512,512]{0,1:T(8,128)}) %all-reduce.4.cloned.1.call-update) | async-done | bytes 1048592 | tf_op jit(solution)/shard_map/psum | solution.py:115
  903.9 2.5 dot_general.28
  906.4 55.9 %all-reduce.6.cloned.1.call-done = f32[512,512]{0,1:T(8,128)} async-done(((f32[512,512]{0,1:T(8,128)}), f32[512,512]{0,1:T(8,128)}) %all-reduce.6.cloned.1.call-update) | async-done | bytes 1048592 | tf_op jit(solution)/shard_map/psum | solution.py:115
  962.3 2.6 copy.55
  967.3 11.7 %cholesky.104 = f32[128,128]{1,0:T(8,128)S(1)} custom-call(f32[128,128]{1,0:T(8,128)S(1)} %cholesky.266), custom_call_target="Cholesky" | custom-call | tf_op jit(solution)/shard_map/jit(cholesky)/cholesky | solution.py:116
  979.2 9.8 custom-call.31
  991.5 11.7 %cholesky.217 = f32[128,128]{1,0:T(8,128)S(1)} custom-call(f32[128,128]{1,0:T(8,128)S(1)} %cholesky.270), custom_call_target="Cholesky" | custom-call | tf_op jit(solution)/shard_map/jit(cholesky)/cholesky | solution.py:116
  1003.3 10.0 custom-call.32
  1014.8 11.7 %cholesky.238 = f32[128,128]{1,0:T(8,128)S(1)} custom-call(f32[128,128]{1,0:T(8,128)S(1)} %cholesky.275), custom_call_target="Cholesky" | custom-call | tf_op jit(solution)/shard_map/jit(cholesky)/cholesky | solution.py:116
  1026.6 9.8 custom-call.33
  1037.8 11.7 %cholesky.255 = f32[128,128]{1,0:T(8,128)S(1)} custom-call(f32[128,128]{1,0:T(8,128)S(1)} %convolution_subtract_fusion.5), custom_call_target="Cholesky" | custom-call | tf_op jit(solution)/shard_map/jit(cholesky)/cholesky | solution.py:116
  1055.5 14.1 %while.1 = (s32[]{:T(128)}, f32[512,512]{1,0:T(8,128)}, s32[4,2]{0,1:T(2,128)S(1)}, f32[4,128,128]{2,1,0:T(8,128)}, s32[]{:T(128)}) while((s32[]{:T(128)}, f32[512,512]{1,0:T(8,128)}, s32[4,2]{0,1:T(2,128)S(1)}, f32[4,128,128]{2,1,0:T(8,128)}, s32[]{:T(128)}) %tuple.46), condition=%wide.while_cond, body=%wide.while_body.sunk | while | flops 2 | bytes 132205 | solution.py:118
  1056.1 2.9 bitcast_dynamic-update-slice_fusion.5
  1059.7 2.9 bitcast_dynamic-update-slice_fusion.5
  1063.2 2.9 bitcast_dynamic-update-slice_fusion.5
  1066.8 2.8 bitcast_dynamic-update-slice_fusion.5
  1069.6 40.1 %custom-call.34 = f32[4,128,128]{1,2,0:T(8,128)S(1)} custom-call(f32[4,128,128]{2,1,0:T(8,128)} %get-tuple-element.12), custom_call_target="InvertDiagBlocksLowerTriangular" | custom-call | tf_op jit(solution)/shard_map/jit(_solve_triangular)/triangular_solve | solution.py:118
  1116.4 4.8 fusion.30
  (170 shorter events, 63.7 us)
Async XLA Ops:
  8.1 6.2 copy-start.21
  8.1 8.3 copy-start.20
  8.1 23.5 %copy-start.1 = (f32[2,16,128,128]{3,2,1,0:T(8,128)S(1)}, f32[2,16,128,128]{3,2,1,0:T(8,128)}, u32[]{:S(2)}) copy-start(f32[2,16,128,128]{3,2,1,0:T(8,128)} %param.6) | copy-start | bytes 6291460
  18.6 43.7 %all-to-all-start = ((f32[64,1,1]{2,1,0:T(1,128)}), f32[64,1,1]{2,1,0:T(1,128)S(1)}, u32[]{:S(2)}, u32[]{:S(2)}) async-start(f32[64,1,1]{2,1,0:T(1,128)} %broadcast_in_dim.49), calls=%async_computation | async-start | bytes 65536 | tf_op jit(solution)/shard_map/all_to_all | solution.py:25
  33.1 57.2 %collective-permute-start.1 = (f32[1,16,128,128]{3,2,1,0:T(8,128)}, f32[1,16,128,128]{3,2,1,0:T(8,128)}, u32[]{:S(2)}, u32[]{:S(2)}) collective-permute-start(f32[1,16,128,128]{3,2,1,0:T(8,128)} %get-tuple-element.37), channel_id=1, source_target_pairs={{4,0},{8,4},{12,8},{16,12},{20,16},{24,20},{28,24},{32,28},{36,32}... | collective-permute-start | bytes 3145736 | tf_op jit(solution)/shard_map/ppermute | solution.py:18
  35.8 1.5 copy-start.22
  35.8 54.5 %collective-permute-start = (f32[1,16,128,128]{3,2,1,0:T(8,128)}, f32[1,16,128,128]{3,2,1,0:T(8,128)}, u32[]{:S(2)}, u32[]{:S(2)}) collective-permute-start(f32[1,16,128,128]{3,2,1,0:T(8,128)} %get-tuple-element.38), channel_id=1, source_target_pairs={{0,4},{4,8},{8,12},{12,16},{16,20},{20,24},{24,28},{28,32},{32,36}... | collective-permute-start | bytes 3145736 | tf_op jit(solution)/shard_map/ppermute | solution.py:17
  45.8 3.3 copy-start.6
  49.1 2.3 copy-start.7
  51.4 2.3 copy-start.8
  53.8 1.7 copy-start
  63.5 21.4 %all-to-all-start.1 = ((f32[64,1,1]{2,1,0:T(1,128)}), f32[64,1,1]{2,1,0:T(1,128)S(1)}, u32[]{:S(2)}, u32[]{:S(2)}) async-start(f32[64,1,1]{2,1,0:T(1,128)} %broadcast_in_dim.50), calls=%async_computation.1 | async-start | bytes 65536 | tf_op jit(solution)/shard_map/all_to_all | solution.py:25
  75.5 826.4 %all-reduce.4.cloned.1.call-start = ((), (), s32[]{:S(2)}) async-start(), calls=%async_computation.3 | async-start | bytes 2097152 | tf_op jit(solution)/shard_map/psum | solution.py:115
  131.9 26.2 %collective-permute-start.3 = (f32[1,16,128,128]{3,2,1,0:T(8,128)}, f32[1,16,128,128]{3,2,1,0:T(8,128)}, u32[]{:S(2)}, u32[]{:S(2)}) collective-permute-start(f32[1,16,128,128]{3,2,1,0:T(8,128)} %get-tuple-element.33), channel_id=1, source_target_pairs={{4,0},{8,4},{12,8},{16,12},{20,16},{24,20},{28,24},{32,28},{36,32}... | collective-permute-start | bytes 3145736 | tf_op jit(solution)/shard_map/ppermute | solution.py:18
  133.5 24.7 %collective-permute-start.2 = (f32[1,16,128,128]{3,2,1,0:T(8,128)S(1)}, f32[1,16,128,128]{3,2,1,0:T(8,128)}, u32[]{:S(2)}, u32[]{:S(2)}) collective-permute-start(f32[1,16,128,128]{3,2,1,0:T(8,128)S(1)} %get-tuple-element.34), channel_id=1, source_target_pairs={{0,4},{4,8},{8,12},{12,16},{16,20},{20,24},{24,28},{28,32},{32,36}... | collective-permute-start | bytes 3145736 | tf_op jit(solution)/shard_map/ppermute | solution.py:17
  148.6 3.3 copy-start.14
  151.9 2.3 copy-start.13
  154.2 2.3 copy-start.10
  156.6 2.3 copy-start.2
  170.1 3.3 copy-start.16
  196.6 7.2 copy-start.23
  196.6 7.2 copy-start.4
  199.8 23.4 %collective-permute-start.5 = (f32[1,16,128,128]{3,2,1,0:T(8,128)}, f32[1,16,128,128]{3,2,1,0:T(8,128)}, u32[]{:S(2)}, u32[]{:S(2)}) collective-permute-start(f32[1,16,128,128]{3,2,1,0:T(8,128)} %get-tuple-element.29), channel_id=1, source_target_pairs={{4,0},{8,4},{12,8},{16,12},{20,16},{24,20},{28,24},{32,28},{36,32}... | collective-permute-start | bytes 3145736 | tf_op jit(solution)/shard_map/ppermute | solution.py:18
  203.6 24.1 %collective-permute-start.4 = (f32[1,16,128,128]{3,2,1,0:T(8,128)}, f32[1,16,128,128]{3,2,1,0:T(8,128)}, u32[]{:S(2)}, u32[]{:S(2)}) collective-permute-start(f32[1,16,128,128]{3,2,1,0:T(8,128)} %get-tuple-element.30), channel_id=1, source_target_pairs={{0,4},{4,8},{8,12},{12,16},{16,20},{20,24},{24,28},{28,32},{32,36}... | collective-permute-start | bytes 3145736 | tf_op jit(solution)/shard_map/ppermute | solution.py:17
  211.9 3.3 copy-start.12
  215.2 2.3 copy-start.11
  217.6 2.3 copy-start.9
  238.9 3.3 copy-start.15
  242.2 2.3 copy-start.3
  300.0 4.5 copy-start.5
  304.6 657.7 %all-reduce.6.cloned.1.call-start = ((), (), s32[]{:S(2)}) async-start(), calls=%async_computation.4 | async-start | bytes 2097152 | tf_op jit(solution)/shard_map/psum | solution.py:115
  962.3 2.6 copy-start.17
  966.3 1.0 copy-start.19
  1055.4 57.2 %copy-start.18 = (f32[512,512]{1,0:T(8,128)S(1)}, f32[512,512]{1,0:T(8,128)}, u32[]{:S(2)}) copy-start(f32[512,512]{1,0:T(8,128)} %fusion.46) | copy-start | bytes 3145732
Sparse Core Ops, SparseCore 0:
  304.7 597.2 all-reduce.3
  904.6 57.6 all-reduce.5
